TPU v7x, 256 devices: a whole 4x4x8 slice. The times are simulated.
256 devices in a mesh: dp: 16 (over z, core), expert: 16 (over y, x).
Axes of the slice: x: 4, y: 4, z: 8, core: 2. Of those that a mesh axis runs over, the one named last changes fastest.
Arguments:
- tokens: bfloat16 [65536, 1024], P(('dp', 'expert')), may hold values from -6 to 6
- cotangent: bfloat16 [65536, 1024], P(('dp', 'expert')), may hold values from -6 to 6
- route_logits: float32 [65536, 2], P(('dp', 'expert')), may hold values from -6 to 6
- expert_ids: int32 [65536, 2], P(('dp', 'expert')), may hold values from 0 to 31, as said below
- slot_pos: int32 [65536, 2], P(('dp', 'expert')), may hold values from 0 to 31, as said below
- w_in: bfloat16 [32, 1024, 1536], P('expert'), may hold values from -0.1875 to 0.1875
- w_down: bfloat16 [32, 768, 1024], P('expert'), may hold values from -0.21875 to 0.21875
Outputs:
- input_grad: bfloat16 [65536, 1024], P(('dp', 'expert'))
- grad_in: float32 [32, 1024, 1536], P('expert', 'dp')
- grad_down: float32 [32, 768, 1024], P('expert', 'dp')
Inputs may be any that keep to these rules, and one draw needn't show every extreme that they name: `expert_ids`: each row names 2 different experts. Within each aligned block of 256 rows (the tokens of one device) no expert is named more than 32 times, and one expert, the same in all blocks, is named exactly 32 times in every block. `slot_pos`: within each aligned block of 256 rows, entries whose matching expert_ids entries name the same expert are distinct.
All inputs are finite; a program needn't handle non-finite values.
Results may differ from a plain program's by a relative error of at most 0.02.
Values may be sent and summed in bfloat16 or wider, within the bound.
A program may use at most 128 MiB of HBM per device.

v0:
```python
import jax
import jax.numpy as jnp
from jax import lax
from jax.sharding import PartitionSpec as P

TOP = 2


def recompute(input_slots, w_in, hidden_width):
    gate = jnp.einsum(
        "ksd,kdf->ksf", input_slots, w_in[:, :, :hidden_width], preferred_element_type=jnp.float32
    )
    upper = jnp.einsum(
        "ksd,kdf->ksf", input_slots, w_in[:, :, hidden_width:], preferred_element_type=jnp.float32
    )
    sigmoid_gate = jax.nn.sigmoid(gate)
    activated = gate * sigmoid_gate
    hidden = (activated * upper).astype(jnp.bfloat16)
    return (gate, upper, sigmoid_gate, activated, hidden)


def per_device(tokens, cotangent, route_logits, expert_ids, slot_pos, w_in, w_down):
    token_count, width = tokens.shape
    local_experts = w_in.shape[0]
    hidden_width = w_down.shape[1]
    n_expert = lax.axis_size("expert")
    n_dp = lax.axis_size("dp")
    experts_all = local_experts * n_expert
    capacity = 2 * TOP * token_count // experts_all
    first = jax.nn.sigmoid(route_logits[:, 0] - route_logits[:, 1])
    combine = (first, 1.0 - first)
    cotangent_wide = cotangent.astype(jnp.float32)
    destination = (expert_ids * capacity + slot_pos).reshape(-1)
    target = expert_ids * (2 * capacity) + slot_pos
    buffer_row = lax.broadcasted_iota(jnp.int32, (experts_all * 2 * capacity, token_count), 0)
    picks = []
    for k in range(TOP):
        picks.append((buffer_row == target[None, :, k]).astype(jnp.bfloat16))
    token_picks = picks[0] + picks[1]
    send = jnp.dot(token_picks, tokens, preferred_element_type=jnp.float32)
    for k in range(TOP):
        scaled = (combine[k][:, None] * cotangent_wide).astype(jnp.bfloat16)
        shifted = (buffer_row == target[None, :, k] + capacity).astype(jnp.bfloat16)
        send = send + jnp.dot(shifted, scaled, preferred_element_type=jnp.float32)
    send = send.astype(jnp.bfloat16).reshape(experts_all, 2, capacity, width)
    got = lax.all_to_all(send, "expert", split_axis=0, concat_axis=0, tiled=True)
    got = got.reshape(n_expert, local_experts, 2, capacity, width)
    got = jnp.transpose(got, (2, 1, 0, 3, 4)).reshape(2, local_experts, n_expert * capacity, width)
    input_slots, cotangent_slots = (got[0], got[1])
    gate, upper, sigmoid_gate, activated, hidden = recompute(input_slots, w_in, hidden_width)
    grad_hidden = jnp.einsum(
        "ksd,kfd->ksf", cotangent_slots, w_down, preferred_element_type=jnp.float32
    )
    term_down = jnp.einsum(
        "ksf,ksd->kfd", hidden, cotangent_slots, preferred_element_type=jnp.float32
    )
    grad_gate = grad_hidden * upper * sigmoid_gate * (1.0 + gate * (1.0 - sigmoid_gate))
    grad_up = grad_hidden * activated
    grad_pair = jnp.concatenate([grad_gate, grad_up], axis=2).astype(jnp.bfloat16)
    term_in = jnp.einsum("ksd,ksf->kdf", input_slots, grad_pair, preferred_element_type=jnp.float32)
    returned = jnp.einsum(
        "ksf,kdf->ksd", grad_pair, w_in, preferred_element_type=jnp.float32
    ).astype(jnp.bfloat16)
    arrived = lax.all_to_all(returned, "expert", split_axis=1, concat_axis=0, tiled=True)
    rows = arrived.reshape(-1, width)[destination].reshape(token_count, TOP, width)
    input_grad = jnp.sum(rows.astype(jnp.float32), axis=1).astype(jnp.bfloat16)
    in_rows, in_cols = (term_in.shape[1], term_in.shape[2])
    down_rows, down_cols = (term_down.shape[1], term_down.shape[2])
    rows_q = down_rows // n_dp
    main = rows_q * down_cols // in_cols
    spare = in_cols - down_cols
    part_in = term_in.astype(jnp.bfloat16).reshape(local_experts, n_dp, in_rows // n_dp, in_cols)
    part_down = term_down.astype(jnp.bfloat16).reshape(local_experts, n_dp, rows_q, down_cols)
    pieces = [part_down[:, :, main:, c : c + spare] for c in range(0, down_cols, spare)]
    packed = jnp.concatenate([part_down[:, :, :main], jnp.concatenate(pieces, axis=2)], axis=3)
    parts = jnp.concatenate([part_in, packed], axis=2).reshape(local_experts, -1, in_cols)
    summed = lax.psum_scatter(parts, "dp", scatter_dimension=1, tiled=True)
    grad_in = summed[:, : in_rows // n_dp].astype(jnp.float32)
    got_down = summed[:, in_rows // n_dp :]
    rest = rows_q - main
    tail = [got_down[:, i * rest : (i + 1) * rest, down_cols:] for i in range(down_cols // spare)]
    grad_down = jnp.concatenate([got_down[:, :, :down_cols], jnp.concatenate(tail, axis=2)], axis=1)
    grad_down = grad_down.astype(jnp.float32)
    return (input_grad, grad_in, grad_down)


def solution(mesh):
    in_specs = (
        P(("dp", "expert"), None),
        P(("dp", "expert"), None),
        P(("dp", "expert"), None),
        P(("dp", "expert"), None),
        P(("dp", "expert"), None),
        P("expert", None, None),
        P("expert", None, None),
    )
    out_specs = (P(("dp", "expert"), None), P("expert", "dp", None), P("expert", "dp", None))
    return jax.shard_map(
        per_device, mesh=mesh, in_specs=in_specs, out_specs=out_specs, check_vma=False
    )
```

profile of v0, /device:TPU:4, one launch (start us, length us, event | category | flops | bytes accessed | tf_op | source)
XLA Modules:
  0.0 174.8 jit_solution(13041412101257724786)
XLA Ops:
  7.2 0.9 multiply_add_fusion
  8.1 2.4 %fusion.13 = f32[2048,1024]{1,0:T(8,128)S(1)} fusion(bf16[256,1024]{1,0:T(8,128)(2,1)} %param.7, s32[256]{0:T(256)S(1)} %bitcast.44, s32[256]{0:T(256)S(1)} %bitcast.42), kind=kOutput, calls=%fused_computation.30 | convolution fusion | flops 1077936128 | bytes 8914944 | tf_op jit(solution)/shard_map/dot_general | solution.py:40
  10.5 1.3 fusion.7
  11.9 2.6 %add_convert_fusion = bf16[2048,1024]{1,0:T(8,128)(2,1)S(1)} fusion(f32[2048,1024]{1,0:T(8,128)S(1)} %fusion.13, f32[2048,1024]{1,0:T(8,128)S(1)} %fusion.7, s32[256]{0:T(256)S(1)} %broadcast_add_fusion, bf16[256,1024]{1,0:T(8,128)(2,1)} %param.8, f32[256]{0:T(256)S(1)} %bitcast.46), kind=kOutput, calls=%fused_computation.2 | convolution fusion | flops 1081344000 | bytes 21497856 | tf_op jit(solution)/shard_map/dot_general | solution.py:44
  14.5 55.5 %all_to_all.20 = bf16[32,2,32,1024]{3,2,1,0:T(8,128)(2,1)S(1)} all-to-all(bf16[32,2,32,1024]{3,2,1,0:T(8,128)(2,1)S(1)} %bitcast.31), channel_id=1, replica_groups=mesh['dp'=16,'expert'=16] {'expert'}, dimensions={0} | all-to-all | bytes 8388608 | tf_op jit(solution)/shard_map/all_to_all | solution.py:46
  70.0 0.8 copy.28
  71.4 1.9 %fusion.32 = f32[2,512,768]{2,1,0:T(8,128)S(1)} fusion(bf16[2,512,1024]{2,1,0:T(8,128)(2,1)S(1)} %bitcast.39, bf16[2,768,1024]{2,1,0:T(8,128)(2,1)S(1)} %copy-done), kind=kOutput, calls=%fused_computation.54 | convolution fusion | flops 1610612736 | bytes 8388608 | tf_op jit(solution)/shard_map/ksd,kfd->ksf/dot_general | solution.py:51
  73.8 1.8 %fusion.3 = f32[2,512,768]{2,1,0:T(8,128)S(1)} fusion(bf16[2,512,1024]{2,1,0:T(8,128)(2,1)S(1)} %bitcast.36, bf16[2,1024,1536]{2,1,0:T(8,128)(2,1)S(1)} %bitcast.49), kind=kOutput, calls=%fused_computation.13 | convolution fusion | flops 1610612736 | bytes 8388608 | tf_op jit(solution)/shard_map/ksd,kdf->ksf/dot_general | solution.py:13
  75.6 3.0 %multiply_convert_fusion.2 = (bf16[2,512,768]{2,1,0:T(8,128)(2,1)S(1)}, bf16[2,512,768]{2,1,0:T(8,128)(2,1)S(1)}, f32[2,512,768]{2,1,0:T(8,128)S(1)}) fusion(f32[2,512,768]{2,1,0:T(8,128)S(1)} %fusion.32, f32[2,512,768]{2,1,0:T(8,128)S(1)} %fusion.3, bf16[2,512,1024]{2,1,0:T(8,128)(2,1)S(1)} %bitcast.37, bf16[2,1024,1536]{2,1,0:T(8,128)(2,1)S(1)} %bitcast.49), kind=kOutput, calls=%fused_computation.8 | convolution fusion | flops 1620836352 | bytes 17825792 | tf_op jit(solution)/shard_map/ksd,kdf->ksf/dot_general | solution.py:10
  78.6 2.0 %convolution_convert_fusion.1 = bf16[2,768,1024]{2,1,0:T(8,128)(2,1)S(1)} fusion(bf16[2,512,1024]{2,1,0:T(8,128)(2,1)S(1)} %bitcast.40, f32[2,512,768]{2,1,0:T(8,128)S(1)} %fusion.3, f32[2,512,768]{2,1,0:T(8,128)S(1)} %get-tuple-element.17), kind=kOutput, calls=%fused_computation.15 | convolution fusion | flops 1616904192 | bytes 11534336 | tf_op jit(solution)/shard_map/ksf,ksd->kfd/dot_general | solution.py:54
  81.0 3.8 %convolution_convert_fusion = bf16[2,1024,1536]{2,1,0:T(8,128)(2,1)S(1)} fusion(bf16[2,512,1024]{2,1,0:T(8,128)(2,1)S(1)} %bitcast.38, bf16[2,512,768]{2,1,0:T(8,128)(2,1)S(1)} %get-tuple-element.6, bf16[2,512,768]{2,1,0:T(8,128)(2,1)S(1)} %get-tuple-element.5), kind=kOutput, calls=%fused_computation.3 | convolution fusion | flops 3230662656 | bytes 11534336 | tf_op jit(solution)/shard_map/ksd,ksf->kdf/dot_general | solution.py:60
  84.8 4.1 %maximum_maximum_fusion = bf16[2,16,96,1536]{3,2,1,0:T(8,128)(2,1)} fusion(bf16[2,16,16,512]{3,2,1,0:T(8,128)(2,1)S(1)} %get-tuple-element.10, bf16[2,16,16,512]{3,2,1,0:T(8,128)(2,1)S(1)} %get-tuple-element.9, bf16[2,16,32,1024]{3,2,1,0:T(8,128)(2,1)S(1)} %slice.74, bf16[2,16,64,1536]{3,2,1,0:T(8,128)(2,1)S(1)} %bitcast.33), kind=kLoop, calls=%fused_computation.1 | loop fusion | flops 37748736 | bytes 18874368 | tf_op jit(solution)/shard_map/concatenate | solution.py:76
  88.8 7.2 %fusion.9 = bf16[2,512,1024]{2,1,0:T(8,128)(2,1)S(1)} fusion(bf16[2,1024,1536]{2,1,0:T(8,128)(2,1)} %param.12, bf16[2,512,768]{2,1,0:T(8,128)(2,1)} %copy-done.5, bf16[2,512,768]{2,1,0:T(8,128)(2,1)} %copy-done.4), kind=kOutput, calls=%fused_computation.24 | convolution fusion | flops 3228565504 | bytes 11534336 | tf_op jit(solution)/shard_map/ksf,kdf->ksd/dot_general | solution.py:61
  96.0 3.5 %copy.20 = bf16[2,512,1024]{2,0,1:T(2,128)(2,1)} copy(bf16[2,512,1024]{2,1,0:T(8,128)(2,1)S(1)} %fusion.9) | data formatting | bytes 4194304 | tf_op jit(solution)/shard_map/convert_element_type | solution.py:63
  99.5 6.2 %all-to-all-start.1 = ((bf16[2,512,1024]{2,0,1:T(2,128)(2,1)}), bf16[2,512,1024]{2,0,1:T(2,128)(2,1)S(1)}, u32[]{:S(2)}, u32[]{:S(2)}) async-start(bf16[2,512,1024]{2,0,1:T(2,128)(2,1)} %copy.20), calls=%async_computation.1 | async-start | bytes 4194304 | tf_op jit(solution)/shard_map/all_to_all | solution.py:64
  106.0 25.2 %all-to-all-done.1 = bf16[2,512,1024]{2,0,1:T(2,128)(2,1)S(1)} async-done(((bf16[2,512,1024]{2,0,1:T(2,128)(2,1)}), bf16[2,512,1024]{2,0,1:T(2,128)(2,1)S(1)}, u32[]{:S(2)}, u32[]{:S(2)}) %all-to-all-start.1) | async-done | bytes 2097184 | tf_op jit(solution)/shard_map/all_to_all | solution.py:64
  131.3 2.0 %copy.21 = bf16[2,16,32,1024]{3,2,0,1:T(8,128)(2,1)} copy(bf16[2,16,32,1024]{3,0,2,1:T(2,128)(2,1)S(1)} %bitcast.32) | data formatting | bytes 4194304 | tf_op jit(solution)/shard_map/all_to_all | solution.py:64
  133.3 5.5 %gather_fusion = bf16[512,1024]{1,0:T(8,128)(2,1)} fusion(bf16[1024,1024]{1,0:T(8,128)(2,1)} %bitcast.27, s32[1024]{0:T(1024)S(1)} %pad_clamp_fusion), kind=kCustom, calls=%fused_computation | custom fusion | bytes 2099200 | tf_op jit(solution)/shard_map/gather | solution.py:65
  138.8 2.3 %reshape.84 = bf16[256,2,1024]{2,1,0:T(2,128)(2,1)} reshape(bf16[512,1024]{1,0:T(8,128)(2,1)} %gather_fusion) | data formatting | bytes 2097152 | tf_op jit(solution)/shard_map/reshape | solution.py:65
  141.1 4.6 %reduce_sum.12 = bf16[256,1024]{1,0:T(8,128)(2,1)} reduce(bf16[256,2,1024]{2,1,0:T(2,128)(2,1)} %reshape.84, bf16[]{:T(256)} %constant.4.clone.1), dimensions={1}, to_apply=%region_0.0 | reduce | flops 262144 | bytes 1572866 | tf_op jit(solution)/shard_map/reduce_sum | solution.py:66
  145.7 17.9 %reduce-scatter.2.cloned.1.call-done = bf16[2,96,1536]{2,1,0:T(8,128)(2,1)} async-done(((bf16[2,1536,1536]{2,1,0:T(8,128)(2,1)}), bf16[2,96,1536]{2,1,0:T(8,128)(2,1)}) %reduce-scatter.2.cloned.1.call-update) | async-done | bytes 589840 | tf_op jit(solution)/shard_map/reduce_scatter | solution.py:77
  164.3 0.9 slice.78
  165.2 0.8 maximum_convert_fusion
  166.0 2.0 %slice_convert_fusion = f32[2,64,1536]{2,1,0:T(8,128)} fusion(bf16[2,96,1536]{2,1,0:T(8,128)(2,1)} %reduce-scatter.2.cloned.1.call-done), kind=kLoop, calls=%fused_computation.37 | loop fusion | flops 196608 | bytes 1179648 | tf_op jit(solution)/shard_map/convert_element_type | solution.py:78
  (31 shorter events, 2.5 us)
Async XLA Ops:
  7.2 64.2 %copy-start = (bf16[2,768,1024]{2,1,0:T(8,128)(2,1)S(1)}, bf16[2,768,1024]{2,1,0:T(8,128)(2,1)}, u32[]{:S(2)}) copy-start(bf16[2,768,1024]{2,1,0:T(8,128)(2,1)} %param.13) | copy-start | bytes 9437188
  7.2 156.4 %reduce-scatter.2.cloned.1.call-start = ((), (), s32[]{:S(2)}) async-start(), calls=%async_computation.3 | async-start | bytes 10027008 | tf_op jit(solution)/shard_map/reduce_scatter | solution.py:77
  8.1 2.4 %copy-start.3 = (f32[256,2]{0,1:T(2,128)S(1)}, f32[256,2]{0,1:T(2,128)}, u32[]{:S(2)}) copy-start(f32[256,2]{0,1:T(2,128)} %param.9) | copy-start | bytes 6148
  8.1 2.4 %copy-start.2 = (bf16[256,1024]{1,0:T(8,128)(2,1)S(1)}, bf16[256,1024]{1,0:T(8,128)(2,1)}, u32[]{:S(2)}) copy-start(bf16[256,1024]{1,0:T(8,128)(2,1)} %param.8) | copy-start | bytes 1572868
  70.8 2.5 %slice-start = ((s8[6291456]{0:T(1024)(128)(4,1)}), s8[2097152]{0:T(1024)(128)(4,1)S(1)}, s32[]{:S(2)}) async-start(s8[6291456]{0:T(1024)(128)(4,1)} %bitcast.48), calls=%async_computation.4 | async-start | bytes 4194304
  71.4 2.4 %slice-start.1 = ((s8[6291456]{0:T(1024)(128)(4,1)}), s8[4194304]{0:T(1024)(128)(4,1)S(1)}, s32[]{:S(2)}) async-start(s8[6291456]{0:T(1024)(128)(4,1)} %bitcast.48), calls=%async_computation.5 | async-start | bytes 8388608
  78.6 2.4 %copy-start.4 = (bf16[2,512,768]{2,1,0:T(8,128)(2,1)}, bf16[2,512,768]{2,1,0:T(8,128)(2,1)S(1)}, u32[]{:S(2)}) copy-start(bf16[2,512,768]{2,1,0:T(8,128)(2,1)S(1)} %get-tuple-element.5) | copy-start | bytes 4718596
  78.6 2.4 %copy-start.5 = (bf16[2,512,768]{2,1,0:T(8,128)(2,1)}, bf16[2,512,768]{2,1,0:T(8,128)(2,1)S(1)}, u32[]{:S(2)}) copy-start(bf16[2,512,768]{2,1,0:T(8,128)(2,1)S(1)} %get-tuple-element.6) | copy-start | bytes 4718596
  99.5 31.8 %all-to-all-start.1 = ((bf16[2,512,1024]{2,0,1:T(2,128)(2,1)}), bf16[2,512,1024]{2,0,1:T(2,128)(2,1)S(1)}, u32[]{:S(2)}, u32[]{:S(2)}) async-start(bf16[2,512,1024]{2,0,1:T(2,128)(2,1)} %copy.20), calls=%async_computation.1 | async-start | bytes 4194304 | tf_op jit(solution)/shard_map/all_to_all | solution.py:64
  133.3 34.7 %copy-start.1 = (bf16[2,768,1024]{2,1,0:T(8,128)(2,1)S(1)}, bf16[2,768,1024]{2,1,0:T(8,128)(2,1)}, u32[]{:S(2)}) copy-start(bf16[2,768,1024]{2,1,0:T(8,128)(2,1)} %param.13) | copy-start | bytes 9437188
Sparse Core Ops, SparseCore 0:
  88.9 74.5 reduce-scatter.1
where the time goes:
time: 175 us
  blocking collectives  55.5 us (32%)
  waiting for transfers between devices  43.1 us (25%)
  matrix products  26 us (15%)
  local copies, waits for them, and re-layouts  17.4 us (10%)
  between operations  14.3 us (8%)
  other arithmetic  12.3 us (7%)
  starting transfers between devices  6.27 us (4%)
    all_to_all x1, blocking collectives, per_device(): lax.all_to_all(send, 'expert', split_axis=0, concat_axis=0, tiled=True)  55.5 us
    all_to_all x1, waiting for transfers between devices, per_device(): lax.all_to_all(returned, 'expert', split_axis=1, concat_axis=0, tiled=True)  25.2 us
    reduce_scatter x1, waiting for transfers between devices, per_device(): summed = lax.psum_scatter(parts, 'dp', scatter_dimension=1, tiled=True)  17.9 us
    dot_general x1, matrix products, per_device(): jnp.einsum('ksf,kdf->ksd', grad_pair, w_in, preferred_element_type=jnp.fl...  7.19 us
    all_to_all x1, starting transfers between devices, per_device(): lax.all_to_all(returned, 'expert', split_axis=1, concat_axis=0, tiled=True)  6.23 us
    gather x1, local copies, waits for them, and re-layouts, per_device(): arrived.reshape(-1, width)[destination].reshape(token_count, TOP, width)  5.53 us
    reduce_sum x1, other arithmetic, per_device(): input_grad = jnp.sum(rows.astype(jnp.float32), axis=1).astype(jnp.bfloat16)  4.59 us
    concatenate x1, other arithmetic, per_device(): jnp.concatenate([part_in, packed], axis=2)  4.05 us
  transfers between devices with their start and end apart: 2, of which 2 were waited for; matrix products, arithmetic and copies ran while one was open for 14% of the time, Pallas kernels for 0%

commit v1 on v0

--- a/solution.py
+++ b/solution.py
@@ -4,6 +4,17 @@
 from jax.sharding import PartitionSpec as P
 
 TOP = 2
+
+
+def in_blocks(value, dim, devices):
+    before, after = (value.shape[:dim], value.shape[dim + 1 :])
+    return jnp.moveaxis(value.reshape(*before, devices, -1, *after), dim, 0)
+
+
+def in_order(tiles, dim):
+    tiles = jnp.moveaxis(tiles, 0, dim)
+    lengths = tiles.shape
+    return tiles.reshape(*lengths[:dim], lengths[dim] * lengths[dim + 1], *lengths[dim + 2 :])
 
 
 def recompute(input_slots, w_in, hidden_width):
@@ -61,7 +72,14 @@
     returned = jnp.einsum(
         "ksf,kdf->ksd", grad_pair, w_in, preferred_element_type=jnp.float32
     ).astype(jnp.bfloat16)
-    arrived = lax.all_to_all(returned, "expert", split_axis=1, concat_axis=0, tiled=True)
+    size, index = (lax.axis_size("expert"), lax.axis_index("expert"))
+    parts_2 = in_blocks(returned, 1, size)
+    outs = [parts_2[index]]
+    for step in range(1, size):
+        sent = parts_2[index ^ step]
+        outs.append(lax.ppermute(sent, "expert", [(i_2, i_2 ^ step) for i_2 in range(size)]))
+    parts_2 = jnp.stack(outs)[index ^ jnp.arange(size)]
+    arrived = in_order(parts_2, 0)
     rows = arrived.reshape(-1, width)[destination].reshape(token_count, TOP, width)
     input_grad = jnp.sum(rows.astype(jnp.float32), axis=1).astype(jnp.bfloat16)
     in_rows, in_cols = (term_in.shape[1], term_in.shape[2])

time: 175 us -> 175 us (level)
  waiting for transfers between devices: 43.1 us -> 14.2 us
  starting transfers between devices: 6.27 us -> 28.1 us
  local copies, waits for them, and re-layouts: 17.4 us -> 23.9 us
    ppermute x0 -> x15, starting transfers between devices: none -> 28.1 us  [per_device(): lax.ppermute(sent, 'expert', [(i_2, i_2 ^ step) for i_2 in range(size)])]
    all_to_all x1 -> x0, waiting for transfers between devices: 25.2 us -> none  [per_device(): lax.all_to_all(returned, 'expert', split_axis=1, concat_axis=0, tiled=True)]
    unnamed x16 -> x31, local copies, waits for them, and re-layouts: 0.48 us -> 11.4 us
    reduce_scatter x1, waiting for transfers between devices: 17.9 us -> 10.6 us  [per_device(): summed = lax.psum_scatter(parts, 'dp', scatter_dimension=1, tiled=True)]
    all_to_all x1 -> x0, starting transfers between devices: 6.23 us -> none  [per_device(): lax.all_to_all(returned, 'expert', split_axis=1, concat_axis=0, tiled=True)]
    ppermute x0 -> x15, waiting for transfers between devices: none -> 3.61 us  [per_device(): lax.ppermute(sent, 'expert', [(i_2, i_2 ^ step) for i_2 in range(size)])]
    convert_element_type x1 -> x0, local copies, waits for them, and re-layouts: 3.47 us -> none  [per_device(): returned = jnp.einsum('ksf,kdf->ksd', grad_pair, w_in, preferred_element_...]
    gather x1, local copies, waits for them, and re-layouts: 5.53 us -> 2.81 us  [per_device(): arrived.reshape(-1, width)[destination].reshape(token_count, TOP, width)]
  transfers between devices with their start and end apart: 2 -> 16, of which waited for: 2 -> 3; matrix products, arithmetic and copies ran while one was open for 14% -> 18% of each run, Pallas kernels for 0% -> 0%
where the time goes in v1:
time: 175 us; the launch traced here: 174 us
  blocking collectives  55.5 us (32%)
  starting transfers between devices  28.1 us (16%)
  matrix products  26 us (15%)
  local copies, waits for them, and re-layouts  23.9 us (14%)
  between operations  14.4 us (8%)
  waiting for transfers between devices  14.2 us (8%)
  other arithmetic  12.3 us (7%)
    all_to_all x1, blocking collectives, per_device(): lax.all_to_all(send, 'expert', split_axis=0, concat_axis=0, tiled=True)  55.5 us
    ppermute x15, starting transfers between devices, per_device(): lax.ppermute(sent, 'expert', [(i_2, i_2 ^ step) for i_2 in range(size)])  28.1 us
    unnamed x31, local copies, waits for them, and re-layouts  11.4 us
    reduce_scatter x1, waiting for transfers between devices, per_device(): summed = lax.psum_scatter(parts, 'dp', scatter_dimension=1, tiled=True)  10.6 us
    dot_general x1, matrix products, per_device(): jnp.einsum('ksf,kdf->ksd', grad_pair, w_in, preferred_element_type=jnp.fl...  7.19 us
    reduce_sum x1, other arithmetic, per_device(): input_grad = jnp.sum(rows.astype(jnp.float32), axis=1).astype(jnp.bfloat16)  4.58 us
    concatenate x1, other arithmetic, per_device(): jnp.concatenate([part_in, packed], axis=2)  4.07 us
    dot_general x2, matrix products, per_device(): send = send + jnp.dot(shifted, scaled, preferred_element_type=jnp.float32)  3.95 us
  transfers between devices with their start and end apart: 16, of which 3 were waited for; matrix products, arithmetic and copies ran while one was open for 18% of the time, Pallas kernels for 0%

profile of v1, /device:TPU:4, one launch (start us, length us, event | category | flops | bytes accessed | tf_op | source)
XLA Modules:
  0.0 174.5 jit_solution(10992559125790744478)
XLA Ops:
  8.1 2.4 %fusion.13 = f32[2048,1024]{1,0:T(8,128)S(1)} fusion(bf16[256,1024]{1,0:T(8,128)(2,1)} %param.7, s32[256]{0:T(256)S(1)} %bitcast.107, s32[256]{0:T(256)S(1)} %bitcast.105), kind=kOutput, calls=%fused_computation.31 | convolution fusion | flops 1077936128 | bytes 8914944 | tf_op jit(solution)/shard_map/dot_general | solution.py:51
  11.9 2.6 %add_convert_fusion = bf16[2048,1024]{1,0:T(8,128)(2,1)S(1)} fusion(f32[2048,1024]{1,0:T(8,128)S(1)} %fusion.13, f32[2048,1024]{1,0:T(8,128)S(1)} %fusion.7, s32[256]{0:T(256)S(1)} %broadcast_add_fusion, bf16[256,1024]{1,0:T(8,128)(2,1)} %param.8, f32[256]{0:T(256)S(1)} %bitcast.109), kind=kOutput, calls=%fused_computation.3 | convolution fusion | flops 1081344000 | bytes 21497856 | tf_op jit(solution)/shard_map/dot_general | solution.py:55
  14.5 55.5 %all_to_all.5 = bf16[32,2,32,1024]{3,2,1,0:T(8,128)(2,1)S(1)} all-to-all(bf16[32,2,32,1024]{3,2,1,0:T(8,128)(2,1)S(1)} %bitcast.93), channel_id=1, replica_groups=mesh['dp'=16,'expert'=16] {'expert'}, dimensions={0} | all-to-all | bytes 8388608 | tf_op jit(solution)/shard_map/all_to_all | solution.py:57
  71.1 1.9 %fusion.33 = f32[2,512,768]{2,1,0:T(8,128)S(1)} fusion(bf16[2,512,1024]{2,1,0:T(8,128)(2,1)S(1)} %bitcast.102, bf16[2,768,1024]{2,1,0:T(8,128)(2,1)S(1)} %copy-done), kind=kOutput, calls=%fused_computation.89 | convolution fusion | flops 1610612736 | bytes 8388608 | tf_op jit(solution)/shard_map/ksd,kfd->ksf/dot_general | solution.py:62
  73.4 1.8 %fusion.3 = f32[2,512,768]{2,1,0:T(8,128)S(1)} fusion(bf16[2,512,1024]{2,1,0:T(8,128)(2,1)S(1)} %bitcast.99, bf16[2,1024,1536]{2,1,0:T(8,128)(2,1)S(1)} %bitcast.112), kind=kOutput, calls=%fused_computation.14 | convolution fusion | flops 1610612736 | bytes 8388608 | tf_op jit(solution)/shard_map/ksd,kdf->ksf/dot_general | solution.py:24
  75.2 3.0 %multiply_convert_fusion.2 = (bf16[2,512,768]{2,1,0:T(8,128)(2,1)S(1)}, bf16[2,512,768]{2,1,0:T(8,128)(2,1)S(1)}, f32[2,512,768]{2,1,0:T(8,128)S(1)}) fusion(f32[2,512,768]{2,1,0:T(8,128)S(1)} %fusion.33, f32[2,512,768]{2,1,0:T(8,128)S(1)} %fusion.3, bf16[2,512,1024]{2,1,0:T(8,128)(2,1)S(1)} %bitcast.100, bf16[2,1024,1536]{2,1,0:T(8,128)(2,1)S(1)} %bitcast.112), kind=kOutput, calls=%fused_computation.9 | convolution fusion | flops 1620836352 | bytes 17825792 | tf_op jit(solution)/shard_map/ksd,kdf->ksf/dot_general | solution.py:21
  78.3 2.1 %convolution_convert_fusion.1 = bf16[2,768,1024]{2,1,0:T(8,128)(2,1)S(1)} fusion(bf16[2,512,1024]{2,1,0:T(8,128)(2,1)S(1)} %bitcast.103, f32[2,512,768]{2,1,0:T(8,128)S(1)} %fusion.3, f32[2,512,768]{2,1,0:T(8,128)S(1)} %get-tuple-element.32), kind=kOutput, calls=%fused_computation.16 | convolution fusion | flops 1616904192 | bytes 11534336 | tf_op jit(solution)/shard_map/ksf,ksd->kfd/dot_general | solution.py:65
  80.7 3.8 %convolution_convert_fusion = bf16[2,1024,1536]{2,1,0:T(8,128)(2,1)S(1)} fusion(bf16[2,512,1024]{2,1,0:T(8,128)(2,1)S(1)} %bitcast.101, bf16[2,512,768]{2,1,0:T(8,128)(2,1)S(1)} %get-tuple-element.6, bf16[2,512,768]{2,1,0:T(8,128)(2,1)S(1)} %get-tuple-element.5), kind=kOutput, calls=%fused_computation.4 | convolution fusion | flops 3230662656 | bytes 11534336 | tf_op jit(solution)/shard_map/ksd,ksf->kdf/dot_general | solution.py:71
  84.5 4.1 %maximum_maximum_fusion = bf16[2,16,96,1536]{3,2,1,0:T(8,128)(2,1)} fusion(bf16[2,16,16,512]{3,2,1,0:T(8,128)(2,1)S(1)} %get-tuple-element.10, bf16[2,16,16,512]{3,2,1,0:T(8,128)(2,1)S(1)} %get-tuple-element.9, bf16[2,16,32,1024]{3,2,1,0:T(8,128)(2,1)S(1)} %slice.76, bf16[2,16,64,1536]{3,2,1,0:T(8,128)(2,1)S(1)} %bitcast.94), kind=kLoop, calls=%fused_computation.2 | loop fusion | flops 37748736 | bytes 18874368 | tf_op jit(solution)/shard_map/concatenate | solution.py:94
  89.0 7.2 %fusion.9 = bf16[2,512,1024]{2,1,0:T(8,128)(2,1)S(1)} fusion(bf16[2,1024,1536]{2,1,0:T(8,128)(2,1)} %param.12, bf16[2,512,768]{2,1,0:T(8,128)(2,1)} %copy-done.5, bf16[2,512,768]{2,1,0:T(8,128)(2,1)} %copy-done.4), kind=kOutput, calls=%fused_computation.25 | convolution fusion | flops 3228565504 | bytes 11534336 | tf_op jit(solution)/shard_map/ksf,kdf->ksd/dot_general | solution.py:72
  98.4 2.1 %collective-permute-start.1 = (bf16[2,32,1024]{2,1,0:T(8,128)(2,1)}, bf16[2,32,1024]{2,1,0:T(8,128)(2,1)S(1)}, u32[]{:S(2)}, u32[]{:S(2)}) collective-permute-start(bf16[2,32,1024]{2,1,0:T(8,128)(2,1)} %get-tuple-element.24), channel_id=1, source_target_pairs={{0,2},{1,3},{2,0},{3,1},{4,6},{5,7},{6,4},{7,5},{8,10},{9,11},{10,... | collective-permute-start | bytes 393224 | tf_op jit(solution)/shard_map/ppermute | solution.py:80
  101.4 3.2 %collective-permute-start.4 = (bf16[2,32,1024]{2,1,0:T(8,128)(2,1)S(1)}, bf16[2,32,1024]{2,1,0:T(8,128)(2,1)S(1)}, u32[]{:S(2)}, u32[]{:S(2)}) collective-permute-start(bf16[2,32,1024]{2,1,0:T(8,128)(2,1)S(1)} %get-tuple-element.21), channel_id=1, source_target_pairs={{0,5},{1,4},{2,7},{3,6},{4,1},{5,0},{6,3},{7,2},{8,13},{9,12},{10,... | collective-permute-start | bytes 393224 | tf_op jit(solution)/shard_map/ppermute | solution.py:80
  106.8 1.6 bitcast_dynamic-update-slice_fusion.14
  109.5 1.9 %collective-permute-start.7 = (bf16[2,32,1024]{2,1,0:T(8,128)(2,1)S(1)}, bf16[2,32,1024]{2,1,0:T(8,128)(2,1)S(1)}, u32[]{:S(2)}, u32[]{:S(2)}) collective-permute-start(bf16[2,32,1024]{2,1,0:T(8,128)(2,1)S(1)} %get-tuple-element.18), channel_id=1, source_target_pairs={{0,8},{1,9},{2,10},{3,11},{4,12},{5,13},{6,14},{7,15},{8,0},{9,1},... | collective-permute-start | bytes 393224 | tf_op jit(solution)/shard_map/ppermute | solution.py:80
  112.0 4.7 %collective-permute-start.8 = (bf16[2,32,1024]{2,1,0:T(8,128)(2,1)S(1)}, bf16[2,32,1024]{2,1,0:T(8,128)(2,1)S(1)}, u32[]{:S(2)}, u32[]{:S(2)}) collective-permute-start(bf16[2,32,1024]{2,1,0:T(8,128)(2,1)S(1)} %get-tuple-element.17), channel_id=1, source_target_pairs={{0,9},{1,8},{2,11},{3,10},{4,13},{5,12},{6,15},{7,14},{8,1},{9,0},... | collective-permute-start | bytes 393224 | tf_op jit(solution)/shard_map/ppermute | solution.py:80
  121.2 1.8 %collective-permute-start.11 = (bf16[2,32,1024]{2,1,0:T(8,128)(2,1)S(1)}, bf16[2,32,1024]{2,1,0:T(8,128)(2,1)S(1)}, u32[]{:S(2)}, u32[]{:S(2)}) collective-permute-start(bf16[2,32,1024]{2,1,0:T(8,128)(2,1)S(1)} %get-tuple-element.14), channel_id=1, source_target_pairs={{0,12},{1,13},{2,14},{3,15},{4,8},{5,9},{6,10},{7,11},{8,4},{9,5},... | collective-permute-start | bytes 393224 | tf_op jit(solution)/shard_map/ppermute | solution.py:80
  123.6 5.5 %collective-permute-start.12 = (bf16[2,32,1024]{2,1,0:T(8,128)(2,1)S(1)}, bf16[2,32,1024]{2,1,0:T(8,128)(2,1)S(1)}, u32[]{:S(2)}, u32[]{:S(2)}) collective-permute-start(bf16[2,32,1024]{2,1,0:T(8,128)(2,1)S(1)} %get-tuple-element.13), channel_id=1, source_target_pairs={{0,13},{1,12},{2,15},{3,14},{4,9},{5,8},{6,11},{7,10},{8,5},{9,4},... | collective-permute-start | bytes 393224 | tf_op jit(solution)/shard_map/ppermute | solution.py:80
  135.6 2.9 %collective-permute-done.13 = bf16[2,32,1024]{2,1,0:T(8,128)(2,1)S(1)} collective-permute-done((bf16[2,32,1024]{2,1,0:T(8,128)(2,1)S(1)}, bf16[2,32,1024]{2,1,0:T(8,128)(2,1)S(1)}, u32[]{:S(2)}, u32[]{:S(2)}) %collective-permute-start.13) | collective-permute-done | bytes 131104 | tf_op jit(solution)/shard_map/ppermute | solution.py:80
  140.5 2.3 %gather_fusion = bf16[16,2,32,1024]{3,2,1,0:T(8,128)(2,1)S(1)} fusion(bf16[16,2,32,1024]{3,2,1,0:T(8,128)(2,1)} %bitcast_dynamic-update-slice_fusion, s32[1024]{0:T(1024)S(1)} %pad_clamp_fusion.1), kind=kCustom, calls=%fused_computation | custom fusion | bytes 4194368 | tf_op jit(solution)/shard_map/gather | solution.py:81
  142.8 2.8 %gather_fusion.1 = bf16[512,1024]{1,0:T(8,128)(2,1)} fusion(bf16[1024,1024]{1,0:T(8,128)(2,1)S(1)} %bitcast.89, s32[1024]{0:T(1024)S(1)} %pad_clamp_fusion), kind=kCustom, calls=%fused_computation.1 | custom fusion | bytes 2099200 | tf_op jit(solution)/shard_map/gather | solution.py:83
  145.6 2.4 %reshape.130 = bf16[256,2,1024]{2,1,0:T(2,128)(2,1)} reshape(bf16[512,1024]{1,0:T(8,128)(2,1)} %gather_fusion.1) | data formatting | bytes 2097152 | tf_op jit(solution)/shard_map/reshape | solution.py:83
  148.0 4.6 %reduce_sum.12 = bf16[256,1024]{1,0:T(8,128)(2,1)} reduce(bf16[256,2,1024]{2,1,0:T(2,128)(2,1)} %reshape.130, bf16[]{:T(256)} %constant.18.clone.1), dimensions={1}, to_apply=%region_0.0 | reduce | flops 262144 | bytes 1572866 | tf_op jit(solution)/shard_map/reduce_sum | solution.py:84
  152.6 10.6 %reduce-scatter.2.cloned.1.call-done = bf16[2,96,1536]{2,1,0:T(8,128)(2,1)} async-done(((bf16[2,1536,1536]{2,1,0:T(8,128)(2,1)}), bf16[2,96,1536]{2,1,0:T(8,128)(2,1)}) %reduce-scatter.2.cloned.1.call-update) | async-done | bytes 589840 | tf_op jit(solution)/shard_map/reduce_scatter | solution.py:95
  165.7 2.0 %slice_convert_fusion = f32[2,64,1536]{2,1,0:T(8,128)} fusion(bf16[2,96,1536]{2,1,0:T(8,128)(2,1)} %reduce-scatter.2.cloned.1.call-done), kind=kLoop, calls=%fused_computation.38 | loop fusion | flops 196608 | bytes 1179648 | tf_op jit(solution)/shard_map/convert_element_type | solution.py:96
  (77 shorter events, 27.5 us)
Async XLA Ops:
  7.2 63.9 %copy-start = (bf16[2,768,1024]{2,1,0:T(8,128)(2,1)S(1)}, bf16[2,768,1024]{2,1,0:T(8,128)(2,1)}, u32[]{:S(2)}) copy-start(bf16[2,768,1024]{2,1,0:T(8,128)(2,1)} %param.13) | copy-start | bytes 9437188
  7.2 156.0 %reduce-scatter.2.cloned.1.call-start = ((), (), s32[]{:S(2)}) async-start(), calls=%async_computation.2 | async-start | bytes 10027008 | tf_op jit(solution)/shard_map/reduce_scatter | solution.py:95
  8.1 2.4 %copy-start.3 = (f32[256,2]{0,1:T(2,128)S(1)}, f32[256,2]{0,1:T(2,128)}, u32[]{:S(2)}) copy-start(f32[256,2]{0,1:T(2,128)} %param.9) | copy-start | bytes 6148
  8.1 2.4 %copy-start.2 = (bf16[256,1024]{1,0:T(8,128)(2,1)S(1)}, bf16[256,1024]{1,0:T(8,128)(2,1)}, u32[]{:S(2)}) copy-start(bf16[256,1024]{1,0:T(8,128)(2,1)} %param.8) | copy-start | bytes 1572868
  70.4 2.5 %slice-start = ((s8[6291456]{0:T(1024)(128)(4,1)}), s8[4194304]{0:T(1024)(128)(4,1)S(1)}, s32[]{:S(2)}) async-start(s8[6291456]{0:T(1024)(128)(4,1)} %bitcast.111), calls=%async_computation.3 | async-start | bytes 8388608
  71.0 2.4 %slice-start.1 = ((s8[6291456]{0:T(1024)(128)(4,1)}), s8[2097152]{0:T(1024)(128)(4,1)S(1)}, s32[]{:S(2)}) async-start(s8[6291456]{0:T(1024)(128)(4,1)} %bitcast.111), calls=%async_computation.4 | async-start | bytes 4194304
  78.2 2.4 %copy-start.4 = (bf16[2,512,768]{2,1,0:T(8,128)(2,1)}, bf16[2,512,768]{2,1,0:T(8,128)(2,1)S(1)}, u32[]{:S(2)}) copy-start(bf16[2,512,768]{2,1,0:T(8,128)(2,1)S(1)} %get-tuple-element.5) | copy-start | bytes 4718596
  78.2 2.4 %copy-start.5 = (bf16[2,512,768]{2,1,0:T(8,128)(2,1)}, bf16[2,512,768]{2,1,0:T(8,128)(2,1)S(1)}, u32[]{:S(2)}) copy-start(bf16[2,512,768]{2,1,0:T(8,128)(2,1)S(1)} %get-tuple-element.6) | copy-start | bytes 4718596
  97.3 8.0 %collective-permute-start = (bf16[2,32,1024]{2,1,0:T(8,128)(2,1)}, bf16[2,32,1024]{2,1,0:T(8,128)(2,1)}, u32[]{:S(2)}, u32[]{:S(2)}) collective-permute-start(bf16[2,32,1024]{2,1,0:T(8,128)(2,1)} %get-tuple-element.25), channel_id=1, source_target_pairs={{0,1},{1,0},{2,3},{3,2},{4,5},{5,4},{6,7},{7,6},{8,9},{9,8},{10,11... | collective-permute-start | bytes 393224 | tf_op jit(solution)/shard_map/ppermute | solution.py:80
  98.4 9.9 %collective-permute-start.1 = (bf16[2,32,1024]{2,1,0:T(8,128)(2,1)}, bf16[2,32,1024]{2,1,0:T(8,128)(2,1)S(1)}, u32[]{:S(2)}, u32[]{:S(2)}) collective-permute-start(bf16[2,32,1024]{2,1,0:T(8,128)(2,1)} %get-tuple-element.24), channel_id=1, source_target_pairs={{0,2},{1,3},{2,0},{3,1},{4,6},{5,7},{6,4},{7,5},{8,10},{9,11},{10,... | collective-permute-start | bytes 393224 | tf_op jit(solution)/shard_map/ppermute | solution.py:80
  100.6 8.9 %collective-permute-start.2 = (bf16[2,32,1024]{2,1,0:T(8,128)(2,1)}, bf16[2,32,1024]{2,1,0:T(8,128)(2,1)S(1)}, u32[]{:S(2)}, u32[]{:S(2)}) collective-permute-start(bf16[2,32,1024]{2,1,0:T(8,128)(2,1)} %get-tuple-element.23), channel_id=1, source_target_pairs={{0,3},{1,2},{2,1},{3,0},{4,7},{5,6},{6,5},{7,4},{8,11},{9,10},{10,... | collective-permute-start | bytes 393224 | tf_op jit(solution)/shard_map/ppermute | solution.py:80
  100.8 11.3 %collective-permute-start.3 = (bf16[2,32,1024]{2,1,0:T(8,128)(2,1)}, bf16[2,32,1024]{2,1,0:T(8,128)(2,1)S(1)}, u32[]{:S(2)}, u32[]{:S(2)}) collective-permute-start(bf16[2,32,1024]{2,1,0:T(8,128)(2,1)} %get-tuple-element.22), channel_id=1, source_target_pairs={{0,4},{1,5},{2,6},{3,7},{4,0},{5,1},{6,2},{7,3},{8,12},{9,13},{10,... | collective-permute-start | bytes 393224 | tf_op jit(solution)/shard_map/ppermute | solution.py:80
  101.4 16.0 %collective-permute-start.4 = (bf16[2,32,1024]{2,1,0:T(8,128)(2,1)S(1)}, bf16[2,32,1024]{2,1,0:T(8,128)(2,1)S(1)}, u32[]{:S(2)}, u32[]{:S(2)}) collective-permute-start(bf16[2,32,1024]{2,1,0:T(8,128)(2,1)S(1)} %get-tuple-element.21), channel_id=1, source_target_pairs={{0,5},{1,4},{2,7},{3,6},{4,1},{5,0},{6,3},{7,2},{8,13},{9,12},{10,... | collective-permute-start | bytes 393224 | tf_op jit(solution)/shard_map/ppermute | solution.py:80
  105.3 14.4 %collective-permute-start.5 = (bf16[2,32,1024]{2,1,0:T(8,128)(2,1)S(1)}, bf16[2,32,1024]{2,1,0:T(8,128)(2,1)S(1)}, u32[]{:S(2)}, u32[]{:S(2)}) collective-permute-start(bf16[2,32,1024]{2,1,0:T(8,128)(2,1)S(1)} %get-tuple-element.20), channel_id=1, source_target_pairs={{0,6},{1,7},{2,4},{3,5},{4,2},{5,3},{6,0},{7,1},{8,14},{9,15},{10,... | collective-permute-start | bytes 393224 | tf_op jit(solution)/shard_map/ppermute | solution.py:80
  108.4 12.8 %collective-permute-start.6 = (bf16[2,32,1024]{2,1,0:T(8,128)(2,1)S(1)}, bf16[2,32,1024]{2,1,0:T(8,128)(2,1)S(1)}, u32[]{:S(2)}, u32[]{:S(2)}) collective-permute-start(bf16[2,32,1024]{2,1,0:T(8,128)(2,1)S(1)} %get-tuple-element.19), channel_id=1, source_target_pairs={{0,7},{1,6},{2,5},{3,4},{4,3},{5,2},{6,1},{7,0},{8,15},{9,14},{10,... | collective-permute-start | bytes 393224 | tf_op jit(solution)/shard_map/ppermute | solution.py:80
  109.5 14.1 %collective-permute-start.7 = (bf16[2,32,1024]{2,1,0:T(8,128)(2,1)S(1)}, bf16[2,32,1024]{2,1,0:T(8,128)(2,1)S(1)}, u32[]{:S(2)}, u32[]{:S(2)}) collective-permute-start(bf16[2,32,1024]{2,1,0:T(8,128)(2,1)S(1)} %get-tuple-element.18), channel_id=1, source_target_pairs={{0,8},{1,9},{2,10},{3,11},{4,12},{5,13},{6,14},{7,15},{8,0},{9,1},... | collective-permute-start | bytes 393224 | tf_op jit(solution)/shard_map/ppermute | solution.py:80
  112.0 17.8 %collective-permute-start.8 = (bf16[2,32,1024]{2,1,0:T(8,128)(2,1)S(1)}, bf16[2,32,1024]{2,1,0:T(8,128)(2,1)S(1)}, u32[]{:S(2)}, u32[]{:S(2)}) collective-permute-start(bf16[2,32,1024]{2,1,0:T(8,128)(2,1)S(1)} %get-tuple-element.17), channel_id=1, source_target_pairs={{0,9},{1,8},{2,11},{3,10},{4,13},{5,12},{6,15},{7,14},{8,1},{9,0},... | collective-permute-start | bytes 393224 | tf_op jit(solution)/shard_map/ppermute | solution.py:80
  117.4 14.7 %collective-permute-start.9 = (bf16[2,32,1024]{2,1,0:T(8,128)(2,1)S(1)}, bf16[2,32,1024]{2,1,0:T(8,128)(2,1)S(1)}, u32[]{:S(2)}, u32[]{:S(2)}) collective-permute-start(bf16[2,32,1024]{2,1,0:T(8,128)(2,1)S(1)} %get-tuple-element.16), channel_id=1, source_target_pairs={{0,10},{1,11},{2,8},{3,9},{4,14},{5,15},{6,12},{7,13},{8,2},{9,3},... | collective-permute-start | bytes 393224 | tf_op jit(solution)/shard_map/ppermute | solution.py:80
  119.6 14.0 %collective-permute-start.10 = (bf16[2,32,1024]{2,1,0:T(8,128)(2,1)S(1)}, bf16[2,32,1024]{2,1,0:T(8,128)(2,1)S(1)}, u32[]{:S(2)}, u32[]{:S(2)}) collective-permute-start(bf16[2,32,1024]{2,1,0:T(8,128)(2,1)S(1)} %get-tuple-element.15), channel_id=1, source_target_pairs={{0,11},{1,10},{2,9},{3,8},{4,15},{5,14},{6,13},{7,12},{8,3},{9,2},... | collective-permute-start | bytes 393224 | tf_op jit(solution)/shard_map/ppermute | solution.py:80
  121.2 13.1 %collective-permute-start.11 = (bf16[2,32,1024]{2,1,0:T(8,128)(2,1)S(1)}, bf16[2,32,1024]{2,1,0:T(8,128)(2,1)S(1)}, u32[]{:S(2)}, u32[]{:S(2)}) collective-permute-start(bf16[2,32,1024]{2,1,0:T(8,128)(2,1)S(1)} %get-tuple-element.14), channel_id=1, source_target_pairs={{0,12},{1,13},{2,14},{3,15},{4,8},{5,9},{6,10},{7,11},{8,4},{9,5},... | collective-permute-start | bytes 393224 | tf_op jit(solution)/shard_map/ppermute | solution.py:80
  123.6 11.3 %collective-permute-start.12 = (bf16[2,32,1024]{2,1,0:T(8,128)(2,1)S(1)}, bf16[2,32,1024]{2,1,0:T(8,128)(2,1)S(1)}, u32[]{:S(2)}, u32[]{:S(2)}) collective-permute-start(bf16[2,32,1024]{2,1,0:T(8,128)(2,1)S(1)} %get-tuple-element.13), channel_id=1, source_target_pairs={{0,13},{1,12},{2,15},{3,14},{4,9},{5,8},{6,11},{7,10},{8,5},{9,4},... | collective-permute-start | bytes 393224 | tf_op jit(solution)/shard_map/ppermute | solution.py:80
  129.8 8.7 %collective-permute-start.13 = (bf16[2,32,1024]{2,1,0:T(8,128)(2,1)S(1)}, bf16[2,32,1024]{2,1,0:T(8,128)(2,1)S(1)}, u32[]{:S(2)}, u32[]{:S(2)}) collective-permute-start(bf16[2,32,1024]{2,1,0:T(8,128)(2,1)S(1)} %get-tuple-element.12), channel_id=1, source_target_pairs={{0,14},{1,15},{2,12},{3,13},{4,10},{5,11},{6,8},{7,9},{8,6},{9,7},... | collective-permute-start | bytes 393224 | tf_op jit(solution)/shard_map/ppermute | solution.py:80
  132.1 7.8 %collective-permute-start.14 = (bf16[2,32,1024]{2,1,0:T(8,128)(2,1)S(1)}, bf16[2,32,1024]{2,1,0:T(8,128)(2,1)S(1)}, u32[]{:S(2)}, u32[]{:S(2)}) collective-permute-start(bf16[2,32,1024]{2,1,0:T(8,128)(2,1)S(1)} %get-tuple-element.11), channel_id=1, source_target_pairs={{0,15},{1,14},{2,13},{3,12},{4,11},{5,10},{6,9},{7,8},{8,7},{9,6},... | collective-permute-start | bytes 393224 | tf_op jit(solution)/shard_map/ppermute | solution.py:80
  145.6 22.0 %copy-start.1 = (bf16[2,768,1024]{2,1,0:T(8,128)(2,1)S(1)}, bf16[2,768,1024]{2,1,0:T(8,128)(2,1)}, u32[]{:S(2)}) copy-start(bf16[2,768,1024]{2,1,0:T(8,128)(2,1)} %param.13) | copy-start | bytes 9437188
Sparse Core Ops, SparseCore 0:
  88.7 74.4 reduce-scatter.1
